TPU v7x, 32 devices: a whole 2x2x4 slice. The times are simulated.
32 devices in a mesh: expert: 4 (over y, x), dp: 8 (over z, core).
Axes of the slice: x: 2, y: 2, z: 4, core: 2. Of those that a mesh axis runs over, the one named last changes fastest.
Arguments:
- tokens: bfloat16 [1024, 5120], P('dp', 'expert'), may hold values from -6 to 6
- routes: int32 [1024, 2], P('dp'), may hold values from 0 to 7, all different within a row; in each aligned block of 128 rows (0 to 127, 128 to 255, ...) at most 48 rows name the same one
- combine: bfloat16 [1024, 2], P('dp'), may hold values from 0.099609375 to 1
- cotangent: bfloat16 [1024, 5120], P('dp', 'expert'), may hold values from -1.5 to 1.5
- w_gate: bfloat16 [8, 5120, 768], P('dp', 'expert'), may hold values from -0.078125 to 0.078125
- w_up: bfloat16 [8, 5120, 768], P('dp', 'expert'), may hold values from -0.078125 to 0.078125
- w_down: bfloat16 [8, 768, 5120], P('dp', None, 'expert'), may hold values from -0.21875 to 0.21875
Outputs:
- token_grad: bfloat16 [1024, 5120], P('dp', 'expert')
- combine_grad: float32 [1024, 2], P('dp')
- grad_gate: bfloat16 [8, 5120, 768], P('dp', 'expert')
- grad_up: bfloat16 [8, 5120, 768], P('dp', 'expert')
- grad_down: bfloat16 [8, 768, 5120], P('dp', None, 'expert')
Inputs may be any that keep to these rules, and one draw needn't show every extreme that they name: `routes`: each token names 2 different experts. The tokens of one group name any one expert at most 48 times, a bound that some block reaches.
All inputs are finite; a program needn't handle non-finite values.
Results may differ from a plain program's by a relative error of at most 0.018.
Values may be sent and summed in bfloat16 or wider, within the bound.
No kernel may reach another device: no remote copies, remote signals or barrier semaphores. Data moves between devices by JAX's collectives and lax.ppermute only.
A program may use at most 64 MiB of HBM per device.

v0:
```python
import jax
import jax.numpy as jnp
from jax import lax
from jax.sharding import PartitionSpec as P


def contract_last(matrix_a, matrix_b):
    return lax.dot_general(
        matrix_a, matrix_b, (((1,), (1,)), ((), ())), preferred_element_type=jnp.float32
    )


def contract_first(matrix_a, matrix_b):
    return lax.dot_general(
        matrix_a, matrix_b, (((0,), (0,)), ((), ())), preferred_element_type=jnp.float32
    )


def swiglu_grads(pre_gate, pre_up, back_hidden, weights):
    sigmas = jax.nn.sigmoid(pre_gate)
    active = pre_gate * sigmas
    hidden = (active * pre_up).astype(jnp.bfloat16)
    scaled = weights[:, None] * back_hidden
    grad_gate_pre = (scaled * pre_up * sigmas * (1.0 + pre_gate * (1.0 - sigmas))).astype(
        jnp.bfloat16
    )
    grad_up_pre = (scaled * active).astype(jnp.bfloat16)
    return (hidden, grad_gate_pre, grad_up_pre)


def body(tokens, routes, combine, cotangent, w_gate, w_up, w_down):
    tok_rows, slice_width = tokens.shape
    top_routes = routes.shape[1]
    experts = lax.axis_size("dp")
    capacity = 3 * tok_rows * top_routes // (2 * experts)
    route_count = tok_rows * top_routes
    slot_total = experts * capacity
    route_flat = routes.reshape(route_count)
    onehot = (route_flat[:, None] == jnp.arange(experts, dtype=jnp.int32)[None, :]).astype(
        jnp.int32
    )
    slot_rank = jnp.sum((jnp.cumsum(onehot, axis=0) - onehot) * onehot, axis=1)
    places = route_flat * capacity + slot_rank
    source = jnp.full((slot_total,), route_count, jnp.int32)
    source = source.at[places].set(jnp.arange(route_count, dtype=jnp.int32))
    blank_row = jnp.zeros((1, slice_width), jnp.bfloat16)
    token_send = jnp.concatenate([tokens, blank_row], axis=0)[source // top_routes]
    cot_send = jnp.concatenate([cotangent, blank_row], axis=0)[source // top_routes]
    comb_send = jnp.concatenate(
        [combine.reshape(route_count), jnp.zeros((1,), jnp.bfloat16)], axis=0
    )[source]
    arrived_tok, arrived_cot, arrived_comb = (
        lax.all_to_all(
            token_send.reshape(experts, capacity, slice_width),
            "dp",
            split_axis=0,
            concat_axis=0,
            tiled=True,
        ),
        lax.all_to_all(
            cot_send.reshape(experts, capacity, slice_width),
            "dp",
            split_axis=0,
            concat_axis=0,
            tiled=True,
        ),
        lax.all_to_all(
            comb_send.reshape(experts, capacity), "dp", split_axis=0, concat_axis=0, tiled=True
        ),
    )
    token_slots = arrived_tok.reshape(slot_total, slice_width)
    cot_slots = arrived_cot.reshape(slot_total, slice_width)
    comb_slots = arrived_comb.reshape(slot_total).astype(jnp.float32)
    gate_mat = w_gate[0]
    up_mat = w_up[0]
    down_mat = w_down[0]
    partials = jnp.stack(
        [
            jnp.dot(token_slots, gate_mat, preferred_element_type=jnp.float32),
            jnp.dot(token_slots, up_mat, preferred_element_type=jnp.float32),
            contract_last(cot_slots, down_mat),
        ],
        axis=1,
    )
    summed = lax.psum_scatter(
        partials.astype(jnp.bfloat16), "expert", scatter_dimension=2, tiled=True
    ).astype(jnp.float32)
    hidden_part, gate_part, up_part = swiglu_grads(
        summed[:, 0], summed[:, 1], summed[:, 2], comb_slots
    )
    slot_comb = jnp.sum(hidden_part.astype(jnp.float32) * summed[:, 2], axis=1)
    joined = lax.all_gather(
        jnp.stack([hidden_part, gate_part, up_part], axis=1), "expert", axis=2, tiled=True
    )
    hidden = joined[:, 0]
    grad_gate_pre = joined[:, 1]
    grad_up_pre = joined[:, 2]
    slot_dx = contract_last(grad_gate_pre, gate_mat) + contract_last(grad_up_pre, up_mat)
    scaled_dy = (comb_slots[:, None] * cot_slots.astype(jnp.float32)).astype(jnp.bfloat16)
    grad_gate = contract_first(token_slots, grad_gate_pre).astype(jnp.bfloat16)[None]
    grad_up = contract_first(token_slots, grad_up_pre).astype(jnp.bfloat16)[None]
    grad_down = contract_first(hidden, scaled_dy).astype(jnp.bfloat16)[None]
    back_dx, back_comb = (
        lax.all_to_all(
            slot_dx.reshape(experts, capacity, slice_width).astype(jnp.bfloat16),
            "dp",
            split_axis=0,
            concat_axis=0,
            tiled=True,
        ).astype(jnp.float32),
        lax.all_to_all(
            slot_comb.reshape(experts, capacity).astype(jnp.bfloat16),
            "dp",
            split_axis=0,
            concat_axis=0,
            tiled=True,
        ).astype(jnp.float32),
    )
    route_dx = back_dx.reshape(slot_total, slice_width)[places].reshape(
        tok_rows, top_routes, slice_width
    )
    token_grad = jnp.sum(route_dx, axis=1).astype(jnp.bfloat16)
    comb_part = back_comb.reshape(slot_total)[places].reshape(tok_rows, top_routes)
    combine_grad = lax.psum(comb_part, "expert")
    return (token_grad, combine_grad, grad_gate, grad_up, grad_down)


def solution(mesh):
    in_specs = (
        P("dp", "expert"),
        P("dp", None),
        P("dp", None),
        P("dp", "expert"),
        P("dp", "expert", None),
        P("dp", "expert", None),
        P("dp", None, "expert"),
    )
    out_specs = (
        P("dp", "expert"),
        P("dp", None),
        P("dp", "expert", None),
        P("dp", "expert", None),
        P("dp", None, "expert"),
    )
    return jax.shard_map(body, mesh=mesh, in_specs=in_specs, out_specs=out_specs, check_vma=False)
```

profile of v0, /device:TPU:0, one launch (start us, length us, event | category | flops | bytes accessed | tf_op | source)
XLA Modules:
  0.0 218.3 jit_solution(15409593457587932573)
XLA Ops:
  10.3 1.4 scatter_custom_fusion
  12.7 2.8 %gather_fusion = bf16[384,1280]{1,0:T(8,128)(2,1)} fusion(bf16[129,1280]{1,0:T(8,128)(2,1)S(1)} %concatenate.9, s32[1024]{0:T(1024)S(1)} %get-tuple-element.26), kind=kCustom, calls=%fused_computation | custom fusion | bytes 1967616 | tf_op jit(solution)/shard_map/gather | solution.py:47
  15.5 6.3 %all-to-all-start = ((bf16[8,48,1280]{2,1,0:T(8,128)(2,1)}), bf16[8,48,1280]{2,1,0:T(8,128)(2,1)S(1)}, u32[]{:S(2)}, u32[]{:S(2)}) async-start(bf16[8,48,1280]{2,1,0:T(8,128)(2,1)} %bitcast.4), calls=%async_computation | async-start | bytes 1966080 | tf_op jit(solution)/shard_map/all_to_all | solution.py:53
  22.8 2.8 %gather_fusion.1 = bf16[384,1280]{1,0:T(8,128)(2,1)} fusion(bf16[129,1280]{1,0:T(8,128)(2,1)S(1)} %concatenate.10, s32[1024]{0:T(1024)S(1)} %get-tuple-element.26), kind=kCustom, calls=%fused_computation.1 | custom fusion | bytes 1967616 | tf_op jit(solution)/shard_map/gather | solution.py:48
  25.6 21.4 %all-to-all-done = bf16[8,48,1280]{2,1,0:T(8,128)(2,1)S(1)} async-done(((bf16[8,48,1280]{2,1,0:T(8,128)(2,1)}), bf16[8,48,1280]{2,1,0:T(8,128)(2,1)S(1)}, u32[]{:S(2)}, u32[]{:S(2)}) %all-to-all-start) | async-done | bytes 983072 | tf_op jit(solution)/shard_map/all_to_all | solution.py:53
  48.0 3.6 %all-to-all-start.1 = ((bf16[8,48,1280]{2,1,0:T(8,128)(2,1)}), bf16[8,48,1280]{2,1,0:T(8,128)(2,1)S(1)}, u32[]{:S(2)}, u32[]{:S(2)}) async-start(bf16[8,48,1280]{2,1,0:T(8,128)(2,1)} %bitcast.107), calls=%async_computation.1 | async-start | bytes 1966080 | tf_op jit(solution)/shard_map/all_to_all | solution.py:60
  51.6 2.9 %fusion.25 = bf16[384,1,768]{2,0,1:T(8,128)(2,1)S(1)} fusion(bf16[384,1280]{1,0:T(8,128)(2,1)} %bitcast.109, bf16[1,1280,768]{2,1,0:T(8,128)(2,1)} %param.12), kind=kOutput, calls=%fused_computation.29 | convolution fusion | flops 755269632 | bytes 3538944 | tf_op jit(solution)/shard_map/dot_general | solution.py:80
  54.5 1.7 fusion.28
  56.2 20.4 %all-to-all-done.1 = bf16[8,48,1280]{2,1,0:T(8,128)(2,1)S(1)} async-done(((bf16[8,48,1280]{2,1,0:T(8,128)(2,1)}), bf16[8,48,1280]{2,1,0:T(8,128)(2,1)S(1)}, u32[]{:S(2)}, u32[]{:S(2)}) %all-to-all-start.1) | async-done | bytes 983072 | tf_op jit(solution)/shard_map/all_to_all | solution.py:60
  76.6 2.9 %fusion.22 = bf16[384,1,768]{2,0,1:T(8,128)(2,1)S(1)} fusion(bf16[384,1280]{1,0:T(8,128)(2,1)S(1)} %bitcast.106, bf16[1,768,1280]{2,1,0:T(8,128)(2,1)} %param.13), kind=kOutput, calls=%fused_computation.28 | convolution fusion | flops 755269632 | bytes 3538944 | tf_op jit(solution)/shard_map/dot_general | solution.py:8
  79.5 1.4 pad_maximum_fusion
  81.0 5.2 %copy.32 = bf16[384,3,768]{0,1,2:T(4,128)(2,1)} copy(bf16[384,3,768]{2,0,1:T(8,128)(2,1)} %pad_maximum_fusion) | data formatting | bytes 3538944
  86.2 3.2 %copy.34 = bf16[96,8,3,384]{3,1,2,0:T(8,128)(2,1)} copy(bf16[96,8,3,384]{3,2,1,0:T(4,128)(2,1)} %bitcast.104) | data formatting | bytes 3538944
  89.7 2.8 %gather_fusion.2 = bf16[384]{0:T(512)(128)(2,1)S(1)} fusion(bf16[257]{0:T(512)(128)(2,1)S(1)} %pad_maximum_fusion.2, s32[1024]{0:T(1024)S(1)} %get-tuple-element.25), kind=kCustom, calls=%fused_computation.2 | custom fusion | bytes 3072 | tf_op jit(solution)/shard_map/gather | solution.py:49
  92.6 7.9 %all_to_all.31 = bf16[8,1,48]{2,1,0:T(2,128)(2,1)S(1)} all-to-all(bf16[8,1,48]{2,1,0:T(2,128)(2,1)S(1)} %all_to_all.25), channel_id=1, replica_groups=mesh['expert'=4,'dp'=8] {'dp'}, dimensions={0} | all-to-all | bytes 1536 | tf_op jit(solution)/shard_map/all_to_all | solution.py:67
  100.6 20.2 %reduce-scatter.4.cloned.1.call-done = bf16[192,1152]{1,0:T(8,128)(2,1)} async-done(((bf16[768,1152]{1,0:T(8,128)(2,1)}), bf16[192,1152]{1,0:T(8,128)(2,1)}) %reduce-scatter.4.cloned.1.call-update) | async-done | bytes 442384
  120.9 1.4 reshape.204
  126.0 2.1 copy.29
  129.0 4.6 %all-to-all-start.4 = ((bf16[8,1,48]{2,1,0:T(2,128)(2,1)}), bf16[8,1,48]{2,1,0:T(2,128)(2,1)S(1)}, u32[]{:S(2)}, u32[]{:S(2)}) async-start(bf16[8,1,48]{2,1,0:T(2,128)(2,1)} %convert_element_type.121), calls=%async_computation.4 | async-start | bytes 8192 | tf_op jit(solution)/shard_map/all_to_all | solution.py:111
  133.6 27.2 %all-gather.2.cloned.1.call-done = bf16[384,3,768]{0,2,1:T(8,128)(2,1)} async-done(((bf16[384,3,192]{0,2,1:T(8,128)(2,1)}), bf16[384,3,768]{0,2,1:T(8,128)(2,1)}) %all-gather.2.cloned.1.call-update) | async-done | bytes 1769488 | tf_op jit(solution)/shard_map/all_gather | solution.py:92
  160.8 2.2 %fusion.9 = f32[384,1280]{1,0:T(8,128)S(1)} fusion(bf16[1,1280,768]{2,1,0:T(8,128)(2,1)S(1)} %copy-done, bf16[384,3,768]{0,2,1:T(8,128)(2,1)} %all-gather.2.cloned.1.call-done), kind=kOutput, calls=%fused_computation.19 | convolution fusion | flops 754974720 | bytes 4521984 | tf_op jit(solution)/shard_map/dot_general | solution.py:8
  163.0 3.1 %fusion.3 = bf16[384,1280]{1,0:T(8,128)(2,1)} fusion(f32[384,1280]{1,0:T(8,128)S(1)} %fusion.9, bf16[1,1280,768]{2,1,0:T(8,128)(2,1)S(1)} %copy-done.9, bf16[384,3,768]{0,2,1:T(8,128)(2,1)} %all-gather.2.cloned.1.call-done), kind=kOutput, calls=%fused_computation.13 | convolution fusion | flops 755957760 | bytes 5505024 | tf_op jit(solution)/shard_map/dot_general | solution.py:8
  166.1 4.7 %all-to-all-start.3 = ((bf16[8,48,1280]{2,1,0:T(8,128)(2,1)}), bf16[8,48,1280]{2,1,0:T(8,128)(2,1)}, u32[]{:S(2)}, u32[]{:S(2)}) async-start(bf16[8,48,1280]{2,1,0:T(8,128)(2,1)} %bitcast.113), calls=%async_computation.3 | async-start | bytes 1966080 | tf_op jit(solution)/shard_map/all_to_all | solution.py:104
  172.1 1.9 gather_fusion.4
  174.2 16.2 %psum.7 = f32[128,2]{1,0:T(8,128)S(1)} all-reduce(f32[128,2]{1,0:T(8,128)S(1)} %reshape.146), channel_id=1, replica_groups=mesh['expert'=4,'dp'=8] {'expert'}, use_global_device_ids=true, to_apply=%region_7.8 | all-reduce | flops 256 | bytes 2048 | tf_op jit(solution)/shard_map/psum | solution.py:124
  191.0 4.0 %fusion = bf16[1,1280,768]{2,1,0:T(8,128)(2,1)} fusion(bf16[384,1280]{1,0:T(8,128)(2,1)} %bitcast.110, bf16[384,3,768]{0,2,1:T(8,128)(2,1)} %all-gather.2.cloned.1.call-done), kind=kOutput, calls=%fused_computation.10 | convolution fusion | flops 755957760 | bytes 3538944 | tf_op jit(solution)/shard_map/dot_general | solution.py:14
  195.0 2.5 %fusion.1 = bf16[1,1280,768]{2,1,0:T(8,128)(2,1)} fusion(bf16[384,1280]{1,0:T(8,128)(2,1)S(1)} %bitcast.112, bf16[384,3,768]{0,2,1:T(8,128)(2,1)S(1)} %copy-done.10), kind=kOutput, calls=%fused_computation.11 | convolution fusion | flops 755957760 | bytes 3538944 | tf_op jit(solution)/shard_map/dot_general | solution.py:14
  197.6 2.4 %fusion.2 = bf16[1,768,1280]{2,1,0:T(8,128)(2,1)} fusion(bf16[384,1280]{1,0:T(8,128)(2,1)S(1)} %bitcast.114, bf16[384,3,768]{0,2,1:T(8,128)(2,1)S(1)} %copy-done.10), kind=kOutput, calls=%fused_computation.12 | convolution fusion | flops 755957760 | bytes 3538944 | tf_op jit(solution)/shard_map/dot_general | solution.py:14
  200.0 2.6 %bitcast_convert_fusion = f32[384,1280]{1,0:T(8,128)} fusion(bf16[8,48,1280]{2,1,0:T(8,128)(2,1)} %all-to-all-done.3), kind=kLoop, calls=%fused_computation.31 | loop fusion | flops 491520 | bytes 2949120 | tf_op jit(solution)/shard_map/reshape | solution.py:119
  202.6 3.3 %gather_fusion.3 = f32[256,1280]{1,0:T(8,128)S(1)} fusion(f32[384,1280]{1,0:T(8,128)} %bitcast_convert_fusion, s32[1024]{0:T(1024)S(1)} %pad_clamp_fusion), kind=kCustom, calls=%fused_computation.3 | custom fusion | bytes 2622464 | tf_op jit(solution)/shard_map/gather | solution.py:119
  206.0 1.8 reshape.145
  207.8 3.6 %reduce_sum.31 = bf16[128,1280]{1,0:T(8,128)(2,1)} reduce(f32[128,2,1280]{2,1,0:T(2,128)} %reshape.145, f32[]{:T(128)} %constant.40.clone.1), dimensions={1}, to_apply=%region_5.6 | reduce | flops 163840 | bytes 1638404 | tf_op jit(solution)/shard_map/reduce_sum | solution.py:122
  (65 shorter events, 13.3 us)
Async XLA Ops:
  7.2 47.3 %copy-start = (bf16[1,1280,768]{2,1,0:T(8,128)(2,1)S(1)}, bf16[1,1280,768]{2,1,0:T(8,128)(2,1)}, u32[]{:S(2)}) copy-start(bf16[1,1280,768]{2,1,0:T(8,128)(2,1)} %param.11) | copy-start | bytes 5898244
  15.5 31.5 %all-to-all-start = ((bf16[8,48,1280]{2,1,0:T(8,128)(2,1)}), bf16[8,48,1280]{2,1,0:T(8,128)(2,1)S(1)}, u32[]{:S(2)}, u32[]{:S(2)}) async-start(bf16[8,48,1280]{2,1,0:T(8,128)(2,1)} %bitcast.4), calls=%async_computation | async-start | bytes 1966080 | tf_op jit(solution)/shard_map/all_to_all | solution.py:53
  47.0 0.9 copy-start.3
  48.0 28.7 %all-to-all-start.1 = ((bf16[8,48,1280]{2,1,0:T(8,128)(2,1)}), bf16[8,48,1280]{2,1,0:T(8,128)(2,1)S(1)}, u32[]{:S(2)}, u32[]{:S(2)}) async-start(bf16[8,48,1280]{2,1,0:T(8,128)(2,1)} %bitcast.107), calls=%async_computation.1 | async-start | bytes 1966080 | tf_op jit(solution)/shard_map/all_to_all | solution.py:60
  51.5 69.4 %reduce-scatter.4.cloned.1.call-start = ((), (), s32[]{:S(2)}) async-start(), calls=%async_computation.7 | async-start | bytes 2211840
  51.6 2.9 %copy-start.4 = (bf16[8,48,1280]{2,1,0:T(8,128)(2,1)S(1)}, bf16[8,48,1280]{2,1,0:T(8,128)(2,1)}, u32[]{:S(2)}) copy-start(bf16[8,48,1280]{2,1,0:T(8,128)(2,1)} %copy-done.3) | copy-start | bytes 2949124
  76.6 2.9 %copy-start.1 = (bf16[8,48,1280]{2,1,0:T(8,128)(2,1)}, bf16[8,48,1280]{2,1,0:T(8,128)(2,1)S(1)}, u32[]{:S(2)}) copy-start(bf16[8,48,1280]{2,1,0:T(8,128)(2,1)S(1)} %all-to-all-done.1) | copy-start | bytes 2949124
  76.6 2.9 %copy-start.7 = (bf16[384,1,768]{2,0,1:T(8,128)(2,1)S(1)}, bf16[384,1,768]{2,0,1:T(8,128)(2,1)}, u32[]{:S(2)}) copy-start(bf16[384,1,768]{2,0,1:T(8,128)(2,1)} %fusion.28) | copy-start | bytes 1769476
  86.1 3.3 %copy-start.8 = (bf16[128,2]{0,1:T(2,128)(2,1)S(1)}, bf16[128,2]{0,1:T(2,128)(2,1)}, u32[]{:S(2)}) copy-start(bf16[128,2]{0,1:T(2,128)(2,1)} %param.9) | copy-start | bytes 1540
  89.4 71.4 %all-gather.2.cloned.1.call-start = ((), (), s32[]{:S(2)}) async-start(), calls=%async_computation.6 | async-start | bytes 2211840 | tf_op jit(solution)/shard_map/all_gather | solution.py:92
  129.0 37.1 %all-to-all-start.4 = ((bf16[8,1,48]{2,1,0:T(2,128)(2,1)}), bf16[8,1,48]{2,1,0:T(2,128)(2,1)S(1)}, u32[]{:S(2)}, u32[]{:S(2)}) async-start(bf16[8,1,48]{2,1,0:T(2,128)(2,1)} %convert_element_type.121), calls=%async_computation.4 | async-start | bytes 8192 | tf_op jit(solution)/shard_map/all_to_all | solution.py:111
  160.8 2.2 %copy-start.9 = (bf16[1,1280,768]{2,1,0:T(8,128)(2,1)S(1)}, bf16[1,1280,768]{2,1,0:T(8,128)(2,1)}, u32[]{:S(2)}) copy-start(bf16[1,1280,768]{2,1,0:T(8,128)(2,1)} %param.12) | copy-start | bytes 5898244
  166.1 4.8 %copy-start.2 = (bf16[8,48,1280]{2,1,0:T(8,128)(2,1)S(1)}, bf16[8,48,1280]{2,1,0:T(8,128)(2,1)}, u32[]{:S(2)}) copy-start(bf16[8,48,1280]{2,1,0:T(8,128)(2,1)} %copy-done.1) | copy-start | bytes 2949124
  166.1 33.9 %all-to-all-start.3 = ((bf16[8,48,1280]{2,1,0:T(8,128)(2,1)}), bf16[8,48,1280]{2,1,0:T(8,128)(2,1)}, u32[]{:S(2)}, u32[]{:S(2)}) async-start(bf16[8,48,1280]{2,1,0:T(8,128)(2,1)} %bitcast.113), calls=%async_computation.3 | async-start | bytes 1966080 | tf_op jit(solution)/shard_map/all_to_all | solution.py:104
  174.2 20.8 %copy-start.5 = (bf16[8,48,1280]{2,1,0:T(8,128)(2,1)S(1)}, bf16[8,48,1280]{2,1,0:T(8,128)(2,1)}, u32[]{:S(2)}) copy-start(bf16[8,48,1280]{2,1,0:T(8,128)(2,1)} %copy-done.3) | copy-start | bytes 2949124
  191.0 4.0 %copy-start.10 = (bf16[384,3,768]{0,2,1:T(8,128)(2,1)S(1)}, bf16[384,3,768]{0,2,1:T(8,128)(2,1)}, u32[]{:S(2)}) copy-start(bf16[384,3,768]{0,2,1:T(8,128)(2,1)} %all-gather.2.cloned.1.call-done) | copy-start | bytes 5308420
  195.0 2.5 %copy-start.6 = (bf16[8,48,1280]{2,1,0:T(8,128)(2,1)S(1)}, bf16[8,48,1280]{2,1,0:T(8,128)(2,1)}, u32[]{:S(2)}) copy-start(bf16[8,48,1280]{2,1,0:T(8,128)(2,1)} %multiply_convert_fusion) | copy-start | bytes 2949124
Sparse Core Ops, SparseCore 0:
  89.5 31.3 reduce-scatter.3
  128.2 32.5 all-gather.1
where the time goes:
time: 219 us; the launch traced here: 218 us
  waiting for transfers between devices  89.4 us (41%)
  local copies, waits for them, and re-layouts  36.5 us (17%)
  blocking collectives  24.1 us (11%)
  matrix products  21.7 us (10%)
  starting transfers between devices  19.3 us (9%)
  between operations  14.3 us (7%)
  other arithmetic  13 us (6%)
    all_gather x1, waiting for transfers between devices, body(): lax.all_gather(jnp.stack([hidden_part, gate_part, up_part], axis=1), 'exp...  27.2 us
    all_to_all x1, waiting for transfers between devices, body(): lax.all_to_all(token_send.reshape(experts, capacity, slice_width), 'dp',...  21.4 us
    all_to_all x1, waiting for transfers between devices, body(): lax.all_to_all(cot_send.reshape(experts, capacity, slice_width), 'dp', sp...  20.4 us
    unnamed x3, waiting for transfers between devices  20.3 us
    psum x1, blocking collectives, body(): combine_grad = lax.psum(comb_part, 'expert')  16.2 us
    unnamed x29, local copies, waits for them, and re-layouts  13.6 us
    dot_general x3, matrix products, contract_first(): lax.dot_general(matrix_a, matrix_b, (((0,), (0,)), ((), ())), preferred_e...  8.94 us
    dot_general x3, matrix products, contract_last(): lax.dot_general(matrix_a, matrix_b, (((1,), (1,)), ((), ())), preferred_e...  8.15 us
  transfers between devices with their start and end apart: 6, of which 4 were waited for; matrix products, arithmetic and copies ran while one was open for 14% of the time, Pallas kernels for 0%

commit v1 on v0

--- a/solution.py
+++ b/solution.py
@@ -2,6 +2,22 @@
 import jax.numpy as jnp
 from jax import lax
 from jax.sharding import PartitionSpec as P
+
+
+def pairwise_exchange(shard, axis, split, join):
+    ways, here = (lax.axis_size(axis), lax.axis_index(axis))
+    width = shard.shape[split] // ways
+    dims = list(shard.shape)
+    dims[split] = width
+    height = dims[join]
+    dims[join] = height * ways
+    full = jnp.zeros(dims, shard.dtype)
+    for mask in range(ways):
+        part = lax.dynamic_slice_in_dim(shard, (here ^ mask) * width, width, axis=split)
+        if mask:
+            part = lax.ppermute(part, axis, [(d, d ^ mask) for d in range(ways)])
+        full = lax.dynamic_update_slice_in_dim(full, part, (here ^ mask) * height, axis=join)
+    return full
 
 
 def contract_last(matrix_a, matrix_b):
@@ -101,12 +117,8 @@
     grad_up = contract_first(token_slots, grad_up_pre).astype(jnp.bfloat16)[None]
     grad_down = contract_first(hidden, scaled_dy).astype(jnp.bfloat16)[None]
     back_dx, back_comb = (
-        lax.all_to_all(
-            slot_dx.reshape(experts, capacity, slice_width).astype(jnp.bfloat16),
-            "dp",
-            split_axis=0,
-            concat_axis=0,
-            tiled=True,
+        pairwise_exchange(
+            slot_dx.reshape(experts, capacity, slice_width).astype(jnp.bfloat16), "dp", 0, 0
         ).astype(jnp.float32),
         lax.all_to_all(
             slot_comb.reshape(experts, capacity).astype(jnp.bfloat16),

time: 219 us -> 208 us (0.950); the launches traced: 218 us -> 204 us
  waiting for transfers between devices: 89.4 us -> 75.1 us
  matrix products: 21.7 us -> 18.1 us
  starting transfers between devices: 19.3 us -> 22.8 us
    all_gather x1, waiting for transfers between devices: 27.2 us -> 2.67 us  [body(): lax.all_gather(jnp.stack([hidden_part, gate_part, up_part], axis=1), 'exp...]
    ppermute x0 -> x7, starting transfers between devices: none -> 8.19 us  [pairwise_exchange(): part = lax.ppermute(part, axis, [(d, d ^ mask) for d in range(ways)])]
    ppermute x0 -> x7, waiting for transfers between devices: none -> 6.31 us  [pairwise_exchange(): part = lax.ppermute(part, axis, [(d, d ^ mask) for d in range(ways)])]
    all_to_all x1 -> x0, starting transfers between devices: 4.75 us -> none  [body(): lax.all_to_all(slot_dx.reshape(experts, capacity, slice_width).astype(jnp...]
    all_to_all x1, waiting for transfers between devices: 0.01 us -> 4 us  [body(): lax.all_to_all(slot_comb.reshape(experts, capacity).astype(jnp.bfloat16),...]
    unnamed x29 -> x25, local copies, waits for them, and re-layouts: 13.6 us -> 13.7 us
  transfers between devices with their start and end apart: 6 -> 12, of which waited for: 4 -> 8; matrix products, arithmetic and copies ran while one was open for 14% -> 12% of each run, Pallas kernels for 0% -> 0%
where the time goes in v1:
time: 208 us; the launch traced here: 204 us
  waiting for transfers between devices  75.1 us (36%)
  local copies, waits for them, and re-layouts  36.8 us (18%)
  blocking collectives  24.9 us (12%)
  starting transfers between devices  22.8 us (11%)
  matrix products  18.1 us (9%)
  between operations  14.4 us (7%)
  other arithmetic  12.2 us (6%)
    all_to_all x1, waiting for transfers between devices, body(): lax.all_to_all(token_send.reshape(experts, capacity, slice_width), 'dp',...  21.4 us
    all_to_all x1, waiting for transfers between devices, body(): lax.all_to_all(cot_send.reshape(experts, capacity, slice_width), 'dp', sp...  20.4 us
    unnamed x3, waiting for transfers between devices  20.3 us
    psum x1, blocking collectives, body(): combine_grad = lax.psum(comb_part, 'expert')  17 us
    unnamed x25, local copies, waits for them, and re-layouts  13.7 us
    ppermute x7, starting transfers between devices, pairwise_exchange(): part = lax.ppermute(part, axis, [(d, d ^ mask) for d in range(ways)])  8.19 us
    all_to_all x1, blocking collectives, body(): lax.all_to_all(comb_send.reshape(experts, capacity), 'dp', split_axis=0,...  7.92 us
    dot_general x3, matrix products, contract_first(): lax.dot_general(matrix_a, matrix_b, (((0,), (0,)), ((), ())), preferred_e...  7.47 us
  transfers between devices with their start and end apart: 12, of which 8 were waited for; matrix products, arithmetic and copies ran while one was open for 12% of the time, Pallas kernels for 0%

profile of v1, /device:TPU:0, one launch (start us, length us, event | category | flops | bytes accessed | tf_op | source)
XLA Modules:
  0.0 204.3 jit_solution(14806031349254741105)
XLA Ops:
  12.7 2.8 %gather_fusion = bf16[384,1280]{1,0:T(8,128)(2,1)} fusion(bf16[129,1280]{1,0:T(8,128)(2,1)S(1)} %concatenate.9, s32[1024]{0:T(1024)S(1)} %get-tuple-element.34), kind=kCustom, calls=%fused_computation | custom fusion | bytes 1967616 | tf_op jit(solution)/shard_map/gather | solution.py:63
  15.5 6.3 %all-to-all-start = ((bf16[8,48,1280]{2,1,0:T(8,128)(2,1)}), bf16[8,48,1280]{2,1,0:T(8,128)(2,1)S(1)}, u32[]{:S(2)}, u32[]{:S(2)}) async-start(bf16[8,48,1280]{2,1,0:T(8,128)(2,1)} %bitcast.4), calls=%async_computation | async-start | bytes 1966080 | tf_op jit(solution)/shard_map/all_to_all | solution.py:69
  22.8 2.8 %gather_fusion.1 = bf16[384,1280]{1,0:T(8,128)(2,1)} fusion(bf16[129,1280]{1,0:T(8,128)(2,1)S(1)} %concatenate.10, s32[1024]{0:T(1024)S(1)} %get-tuple-element.34), kind=kCustom, calls=%fused_computation.1 | custom fusion | bytes 1967616 | tf_op jit(solution)/shard_map/gather | solution.py:64
  25.6 21.4 %all-to-all-done = bf16[8,48,1280]{2,1,0:T(8,128)(2,1)S(1)} async-done(((bf16[8,48,1280]{2,1,0:T(8,128)(2,1)}), bf16[8,48,1280]{2,1,0:T(8,128)(2,1)S(1)}, u32[]{:S(2)}, u32[]{:S(2)}) %all-to-all-start) | async-done | bytes 983072 | tf_op jit(solution)/shard_map/all_to_all | solution.py:69
  48.0 3.6 %all-to-all-start.1 = ((bf16[8,48,1280]{2,1,0:T(8,128)(2,1)}), bf16[8,48,1280]{2,1,0:T(8,128)(2,1)S(1)}, u32[]{:S(2)}, u32[]{:S(2)}) async-start(bf16[8,48,1280]{2,1,0:T(8,128)(2,1)} %bitcast.107), calls=%async_computation.1 | async-start | bytes 1966080 | tf_op jit(solution)/shard_map/all_to_all | solution.py:76
  51.6 2.9 %fusion.25 = bf16[384,1,768]{2,0,1:T(8,128)(2,1)S(1)} fusion(bf16[384,1280]{1,0:T(8,128)(2,1)} %bitcast.109, bf16[1,1280,768]{2,1,0:T(8,128)(2,1)} %param.12), kind=kOutput, calls=%fused_computation.29 | convolution fusion | flops 755269632 | bytes 3538944 | tf_op jit(solution)/shard_map/dot_general | solution.py:96
  54.5 1.7 fusion.28
  56.2 20.4 %all-to-all-done.1 = bf16[8,48,1280]{2,1,0:T(8,128)(2,1)S(1)} async-done(((bf16[8,48,1280]{2,1,0:T(8,128)(2,1)}), bf16[8,48,1280]{2,1,0:T(8,128)(2,1)S(1)}, u32[]{:S(2)}, u32[]{:S(2)}) %all-to-all-start.1) | async-done | bytes 983072 | tf_op jit(solution)/shard_map/all_to_all | solution.py:76
  76.6 2.9 %fusion.22 = bf16[384,1,768]{2,0,1:T(8,128)(2,1)S(1)} fusion(bf16[384,1280]{1,0:T(8,128)(2,1)S(1)} %bitcast.106, bf16[1,768,1280]{2,1,0:T(8,128)(2,1)} %param.13), kind=kOutput, calls=%fused_computation.28 | convolution fusion | flops 755269632 | bytes 3538944 | tf_op jit(solution)/shard_map/dot_general | solution.py:24
  80.9 5.2 %copy.32 = bf16[384,3,768]{0,1,2:T(4,128)(2,1)} copy(bf16[384,3,768]{2,0,1:T(8,128)(2,1)} %pad_maximum_fusion) | data formatting | bytes 3538944
  86.2 3.2 %copy.34 = bf16[96,8,3,384]{3,1,2,0:T(8,128)(2,1)} copy(bf16[96,8,3,384]{3,2,1,0:T(4,128)(2,1)} %bitcast.104) | data formatting | bytes 3538944
  89.7 2.8 %gather_fusion.2 = bf16[384]{0:T(512)(128)(2,1)S(1)} fusion(bf16[257]{0:T(512)(128)(2,1)S(1)} %pad_maximum_fusion.2, s32[1024]{0:T(1024)S(1)} %get-tuple-element.33), kind=kCustom, calls=%fused_computation.2 | custom fusion | bytes 3072 | tf_op jit(solution)/shard_map/gather | solution.py:65
  92.6 7.9 %all_to_all.26 = bf16[8,1,48]{2,1,0:T(2,128)(2,1)S(1)} all-to-all(bf16[8,1,48]{2,1,0:T(2,128)(2,1)S(1)} %all_to_all.21), channel_id=1, replica_groups=mesh['expert'=4,'dp'=8] {'dp'}, dimensions={0} | all-to-all | bytes 1536 | tf_op jit(solution)/shard_map/all_to_all | solution.py:83
  100.7 20.2 %reduce-scatter.4.cloned.1.call-done = bf16[192,1152]{1,0:T(8,128)(2,1)} async-done(((bf16[768,1152]{1,0:T(8,128)(2,1)}), bf16[192,1152]{1,0:T(8,128)(2,1)}) %reduce-scatter.4.cloned.1.call-update) | async-done | bytes 442384
  126.0 2.1 %copy.29 = bf16[384,3,192]{0,2,1:T(8,128)(2,1)} copy(bf16[384,3,192]{2,0,1:T(8,128)(2,1)} %pad_maximum_fusion.1) | data formatting | bytes 884736 | tf_op jit(solution)/shard_map/stack | solution.py:109
  129.0 4.6 %all-to-all-start.3 = ((bf16[8,1,48]{2,1,0:T(2,128)(2,1)}), bf16[8,1,48]{2,1,0:T(2,128)(2,1)S(1)}, u32[]{:S(2)}, u32[]{:S(2)}) async-start(bf16[8,1,48]{2,1,0:T(2,128)(2,1)} %convert_element_type.121), calls=%async_computation.3 | async-start | bytes 8192 | tf_op jit(solution)/shard_map/all_to_all | solution.py:123
  135.1 4.0 %all-to-all-done.3 = bf16[8,1,48]{2,1,0:T(2,128)(2,1)S(1)} async-done(((bf16[8,1,48]{2,1,0:T(2,128)(2,1)}), bf16[8,1,48]{2,1,0:T(2,128)(2,1)S(1)}, u32[]{:S(2)}, u32[]{:S(2)}) %all-to-all-start.3) | async-done | bytes 800 | tf_op jit(solution)/shard_map/all_to_all | solution.py:123
  139.2 1.9 gather_fusion.4
  141.3 17.0 %psum.7 = f32[128,2]{1,0:T(8,128)S(1)} all-reduce(f32[128,2]{1,0:T(8,128)S(1)} %reshape.146), channel_id=1, replica_groups=mesh['expert'=4,'dp'=8] {'expert'}, use_global_device_ids=true, to_apply=%region_7.8 | all-reduce | flops 256 | bytes 2048 | tf_op jit(solution)/shard_map/psum | solution.py:136
  159.0 2.7 %all-gather.2.cloned.1.call-done = bf16[384,3,768]{0,2,1:T(8,128)(2,1)} async-done(((bf16[384,3,192]{0,2,1:T(8,128)(2,1)}), bf16[384,3,768]{0,2,1:T(8,128)(2,1)}) %all-gather.2.cloned.1.call-update) | async-done | bytes 1769488 | tf_op jit(solution)/shard_map/all_gather | solution.py:108
  161.6 2.2 %fusion.9 = f32[384,1280]{1,0:T(8,128)S(1)} fusion(bf16[1,1280,768]{2,1,0:T(8,128)(2,1)S(1)} %copy-done, bf16[384,3,768]{0,2,1:T(8,128)(2,1)} %all-gather.2.cloned.1.call-done), kind=kOutput, calls=%fused_computation.19 | convolution fusion | flops 754974720 | bytes 4521984 | tf_op jit(solution)/shard_map/dot_general | solution.py:24
  165.1 1.6 collective-permute-start.1
  167.0 2.3 %collective-permute-start.3 = (bf16[1,48,1280]{2,1,0:T(8,128)(2,1)S(1)}, bf16[1,48,1280]{2,1,0:T(8,128)(2,1)S(1)}, u32[]{:S(2)}, u32[]{:S(2)}) collective-permute-start(bf16[1,48,1280]{2,1,0:T(8,128)(2,1)S(1)} %get-tuple-element.26), channel_id=1, source_target_pairs={{0,4},{1,5},{2,6},{3,7},{4,0},{5,1},{6,2},{7,3},{8,12},{9,13},{10,... | collective-permute-start | bytes 368648 | tf_op jit(solution)/shard_map/ppermute | solution.py:18
  169.6 2.5 %fusion = bf16[1,1280,768]{2,1,0:T(8,128)(2,1)} fusion(bf16[384,1280]{1,0:T(8,128)(2,1)S(1)} %bitcast.111, bf16[384,3,768]{0,2,1:T(8,128)(2,1)S(1)} %copy-done.8), kind=kOutput, calls=%fused_computation.10 | convolution fusion | flops 755957760 | bytes 3538944 | tf_op jit(solution)/shard_map/dot_general | solution.py:30
  172.1 2.5 %fusion.1 = bf16[1,1280,768]{2,1,0:T(8,128)(2,1)} fusion(bf16[384,1280]{1,0:T(8,128)(2,1)S(1)} %bitcast.112, bf16[384,3,768]{0,2,1:T(8,128)(2,1)S(1)} %copy-done.8), kind=kOutput, calls=%fused_computation.11 | convolution fusion | flops 755957760 | bytes 3538944 | tf_op jit(solution)/shard_map/dot_general | solution.py:30
  174.6 2.5 %fusion.2 = bf16[1,768,1280]{2,1,0:T(8,128)(2,1)} fusion(bf16[384,1280]{1,0:T(8,128)(2,1)S(1)} %bitcast.113, bf16[384,3,768]{0,2,1:T(8,128)(2,1)S(1)} %copy-done.8), kind=kOutput, calls=%fused_computation.12 | convolution fusion | flops 755957760 | bytes 3538944 | tf_op jit(solution)/shard_map/dot_general | solution.py:30
  177.1 2.8 %collective-permute-start.5 = (bf16[1,48,1280]{2,1,0:T(8,128)(2,1)S(1)}, bf16[1,48,1280]{2,1,0:T(8,128)(2,1)S(1)}, u32[]{:S(2)}, u32[]{:S(2)}) collective-permute-start(bf16[1,48,1280]{2,1,0:T(8,128)(2,1)S(1)} %get-tuple-element.24), channel_id=1, source_target_pairs={{0,6},{1,7},{2,4},{3,5},{4,2},{5,3},{6,0},{7,1},{8,14},{9,15},{10,... | collective-permute-start | bytes 368648 | tf_op jit(solution)/shard_map/ppermute | solution.py:18
  181.1 3.5 %collective-permute-done.5 = bf16[1,48,1280]{2,1,0:T(8,128)(2,1)S(1)} collective-permute-done((bf16[1,48,1280]{2,1,0:T(8,128)(2,1)S(1)}, bf16[1,48,1280]{2,1,0:T(8,128)(2,1)S(1)}, u32[]{:S(2)}, u32[]{:S(2)}) %collective-permute-start.5) | collective-permute-done | bytes 122912 | tf_op jit(solution)/shard_map/ppermute | solution.py:18
  184.7 2.5 %collective-permute-done.6 = bf16[1,48,1280]{2,1,0:T(8,128)(2,1)S(1)} collective-permute-done((bf16[1,48,1280]{2,1,0:T(8,128)(2,1)S(1)}, bf16[1,48,1280]{2,1,0:T(8,128)(2,1)S(1)}, u32[]{:S(2)}, u32[]{:S(2)}) %collective-permute-start.6) | collective-permute-done | bytes 122912 | tf_op jit(solution)/shard_map/ppermute | solution.py:18
  188.7 3.3 %gather_fusion.3 = f32[256,1280]{1,0:T(8,128)S(1)} fusion(f32[384,1280]{1,0:T(8,128)} %bitcast_convert_fusion, s32[1024]{0:T(1024)S(1)} %pad_clamp_fusion), kind=kCustom, calls=%fused_computation.3 | custom fusion | bytes 2622464 | tf_op jit(solution)/shard_map/gather | solution.py:131
  192.0 1.9 reshape.145
  193.8 3.6 %reduce_sum.31 = bf16[128,1280]{1,0:T(8,128)(2,1)} reduce(f32[128,2,1280]{2,1,0:T(2,128)} %reshape.145, f32[]{:T(128)} %constant.59.clone.1), dimensions={1}, to_apply=%region_5.6 | reduce | flops 163840 | bytes 1638404 | tf_op jit(solution)/shard_map/reduce_sum | solution.py:134
  (82 shorter events, 22.4 us)
Async XLA Ops:
  7.2 47.3 %copy-start = (bf16[1,1280,768]{2,1,0:T(8,128)(2,1)S(1)}, bf16[1,1280,768]{2,1,0:T(8,128)(2,1)}, u32[]{:S(2)}) copy-start(bf16[1,1280,768]{2,1,0:T(8,128)(2,1)} %param.11) | copy-start | bytes 5898244
  15.5 31.5 %all-to-all-start = ((bf16[8,48,1280]{2,1,0:T(8,128)(2,1)}), bf16[8,48,1280]{2,1,0:T(8,128)(2,1)S(1)}, u32[]{:S(2)}, u32[]{:S(2)}) async-start(bf16[8,48,1280]{2,1,0:T(8,128)(2,1)} %bitcast.4), calls=%async_computation | async-start | bytes 1966080 | tf_op jit(solution)/shard_map/all_to_all | solution.py:69
  47.0 0.9 copy-start.2
  48.0 28.7 %all-to-all-start.1 = ((bf16[8,48,1280]{2,1,0:T(8,128)(2,1)}), bf16[8,48,1280]{2,1,0:T(8,128)(2,1)S(1)}, u32[]{:S(2)}, u32[]{:S(2)}) async-start(bf16[8,48,1280]{2,1,0:T(8,128)(2,1)} %bitcast.107), calls=%async_computation.1 | async-start | bytes 1966080 | tf_op jit(solution)/shard_map/all_to_all | solution.py:76
  51.5 69.4 %reduce-scatter.4.cloned.1.call-start = ((), (), s32[]{:S(2)}) async-start(), calls=%async_computation.6 | async-start | bytes 2211840
  51.6 2.9 %copy-start.3 = (bf16[8,48,1280]{2,1,0:T(8,128)(2,1)S(1)}, bf16[8,48,1280]{2,1,0:T(8,128)(2,1)}, u32[]{:S(2)}) copy-start(bf16[8,48,1280]{2,1,0:T(8,128)(2,1)} %copy-done.2) | copy-start | bytes 2949124
  76.6 2.9 %copy-start.1 = (bf16[8,48,1280]{2,1,0:T(8,128)(2,1)}, bf16[8,48,1280]{2,1,0:T(8,128)(2,1)S(1)}, u32[]{:S(2)}) copy-start(bf16[8,48,1280]{2,1,0:T(8,128)(2,1)S(1)} %all-to-all-done.1) | copy-start | bytes 2949124
  76.6 2.9 %copy-start.5 = (bf16[384,1,768]{2,0,1:T(8,128)(2,1)S(1)}, bf16[384,1,768]{2,0,1:T(8,128)(2,1)}, u32[]{:S(2)}) copy-start(bf16[384,1,768]{2,0,1:T(8,128)(2,1)} %fusion.28) | copy-start | bytes 1769476
  86.2 3.3 %copy-start.6 = (bf16[128,2]{0,1:T(2,128)(2,1)S(1)}, bf16[128,2]{0,1:T(2,128)(2,1)}, u32[]{:S(2)}) copy-start(bf16[128,2]{0,1:T(2,128)(2,1)} %param.9) | copy-start | bytes 1540
  89.4 72.3 %all-gather.2.cloned.1.call-start = ((), (), s32[]{:S(2)}) async-start(), calls=%async_computation.5 | async-start | bytes 2211840 | tf_op jit(solution)/shard_map/all_gather | solution.py:108
  129.0 10.1 %all-to-all-start.3 = ((bf16[8,1,48]{2,1,0:T(2,128)(2,1)}), bf16[8,1,48]{2,1,0:T(2,128)(2,1)S(1)}, u32[]{:S(2)}, u32[]{:S(2)}) async-start(bf16[8,1,48]{2,1,0:T(2,128)(2,1)} %convert_element_type.121), calls=%async_computation.3 | async-start | bytes 8192 | tf_op jit(solution)/shard_map/all_to_all | solution.py:123
  161.6 2.2 %copy-start.7 = (bf16[1,1280,768]{2,1,0:T(8,128)(2,1)S(1)}, bf16[1,1280,768]{2,1,0:T(8,128)(2,1)}, u32[]{:S(2)}) copy-start(bf16[1,1280,768]{2,1,0:T(8,128)(2,1)} %param.12) | copy-start | bytes 5898244
  161.6 2.2 %copy-start.8 = (bf16[384,3,768]{0,2,1:T(8,128)(2,1)S(1)}, bf16[384,3,768]{0,2,1:T(8,128)(2,1)}, u32[]{:S(2)}) copy-start(bf16[384,3,768]{0,2,1:T(8,128)(2,1)} %all-gather.2.cloned.1.call-done) | copy-start | bytes 5308420
  164.9 4.7 %copy-start.4 = (bf16[8,48,1280]{2,1,0:T(8,128)(2,1)S(1)}, bf16[8,48,1280]{2,1,0:T(8,128)(2,1)}, u32[]{:S(2)}) copy-start(bf16[8,48,1280]{2,1,0:T(8,128)(2,1)} %copy-done.2) | copy-start | bytes 2949124
  165.0 12.0 %collective-permute-start = (bf16[1,48,1280]{2,1,0:T(8,128)(2,1)S(1)}, bf16[1,48,1280]{2,1,0:T(8,128)(2,1)S(1)}, u32[]{:S(2)}, u32[]{:S(2)}) collective-permute-start(bf16[1,48,1280]{2,1,0:T(8,128)(2,1)S(1)} %get-tuple-element.29), channel_id=1, source_target_pairs={{0,1},{1,0},{2,3},{3,2},{4,5},{5,4},{6,7},{7,6},{8,9},{9,8},{10,11... | collective-permute-start | bytes 368648 | tf_op jit(solution)/shard_map/ppermute | solution.py:18
  165.1 14.8 %collective-permute-start.1 = (bf16[1,48,1280]{2,1,0:T(8,128)(2,1)S(1)}, bf16[1,48,1280]{2,1,0:T(8,128)(2,1)S(1)}, u32[]{:S(2)}, u32[]{:S(2)}) collective-permute-start(bf16[1,48,1280]{2,1,0:T(8,128)(2,1)S(1)} %get-tuple-element.28), channel_id=1, source_target_pairs={{0,2},{1,3},{2,0},{3,1},{4,6},{5,7},{6,4},{7,5},{8,10},{9,11},{10,... | collective-permute-start | bytes 368648 | tf_op jit(solution)/shard_map/ppermute | solution.py:18
  166.7 14.1 %collective-permute-start.2 = (bf16[1,48,1280]{2,1,0:T(8,128)(2,1)S(1)}, bf16[1,48,1280]{2,1,0:T(8,128)(2,1)S(1)}, u32[]{:S(2)}, u32[]{:S(2)}) collective-permute-start(bf16[1,48,1280]{2,1,0:T(8,128)(2,1)S(1)} %get-tuple-element.27), channel_id=1, source_target_pairs={{0,3},{1,2},{2,1},{3,0},{4,7},{5,6},{6,5},{7,4},{8,11},{9,10},{10,... | collective-permute-start | bytes 368648 | tf_op jit(solution)/shard_map/ppermute | solution.py:18
  167.0 13.8 %collective-permute-start.3 = (bf16[1,48,1280]{2,1,0:T(8,128)(2,1)S(1)}, bf16[1,48,1280]{2,1,0:T(8,128)(2,1)S(1)}, u32[]{:S(2)}, u32[]{:S(2)}) collective-permute-start(bf16[1,48,1280]{2,1,0:T(8,128)(2,1)S(1)} %get-tuple-element.26), channel_id=1, source_target_pairs={{0,4},{1,5},{2,6},{3,7},{4,0},{5,1},{6,2},{7,3},{8,12},{9,13},{10,... | collective-permute-start | bytes 368648 | tf_op jit(solution)/shard_map/ppermute | solution.py:18
  169.2 11.9 %collective-permute-start.4 = (bf16[1,48,1280]{2,1,0:T(8,128)(2,1)S(1)}, bf16[1,48,1280]{2,1,0:T(8,128)(2,1)S(1)}, u32[]{:S(2)}, u32[]{:S(2)}) collective-permute-start(bf16[1,48,1280]{2,1,0:T(8,128)(2,1)S(1)} %get-tuple-element.25), channel_id=1, source_target_pairs={{0,5},{1,4},{2,7},{3,6},{4,1},{5,0},{6,3},{7,2},{8,13},{9,12},{10,... | collective-permute-start | bytes 368648 | tf_op jit(solution)/shard_map/ppermute | solution.py:18
  177.1 7.6 %collective-permute-start.5 = (bf16[1,48,1280]{2,1,0:T(8,128)(2,1)S(1)}, bf16[1,48,1280]{2,1,0:T(8,128)(2,1)S(1)}, u32[]{:S(2)}, u32[]{:S(2)}) collective-permute-start(bf16[1,48,1280]{2,1,0:T(8,128)(2,1)S(1)} %get-tuple-element.24), channel_id=1, source_target_pairs={{0,6},{1,7},{2,4},{3,5},{4,2},{5,3},{6,0},{7,1},{8,14},{9,15},{10,... | collective-permute-start | bytes 368648 | tf_op jit(solution)/shard_map/ppermute | solution.py:18
  179.9 7.3 %collective-permute-start.6 = (bf16[1,48,1280]{2,1,0:T(8,128)(2,1)S(1)}, bf16[1,48,1280]{2,1,0:T(8,128)(2,1)S(1)}, u32[]{:S(2)}, u32[]{:S(2)}) collective-permute-start(bf16[1,48,1280]{2,1,0:T(8,128)(2,1)S(1)} %get-tuple-element.23), channel_id=1, source_target_pairs={{0,7},{1,6},{2,5},{3,4},{4,3},{5,2},{6,1},{7,0},{8,15},{9,14},{10,... | collective-permute-start | bytes 368648 | tf_op jit(solution)/shard_map/ppermute | solution.py:18
Sparse Core Ops, SparseCore 0:
  89.5 31.3 reduce-scatter.3
  128.2 33.4 all-gather.1
